TPU v7x, 32 devices: a whole 2x2x4 slice. The times are simulated.
32 devices in a mesh: groups: 2 (over x), qrow: 4 (over y, core), kcol: 4 (over z).
Axes of the slice: x: 2, y: 2, z: 4, core: 2. Of those that a mesh axis runs over, the one named last changes fastest.
Arguments:
- queries: bfloat16 [8192, 512], P(('groups', 'qrow', 'kcol')), parts along dimension 0, may hold values from -6 to 6
- keys: bfloat16 [8192, 128], P(('groups', 'kcol', 'qrow')), parts along dimension 0, may hold values from -6 to 6
- values: bfloat16 [8192, 128], P(('groups', 'kcol', 'qrow')), parts along dimension 0, may hold values from -6 to 6
- out_grad: bfloat16 [8192, 512], P(('groups', 'qrow', 'kcol')), parts along dimension 0, may hold values from -6 to 6
- pattern: int32 [64, 10], P('groups'), parts along dimension 0, may hold values from 0 to 31, as said below
Outputs:
- attended: bfloat16 [8192, 512], P(('groups', 'qrow', 'kcol')), parts along dimension 0
- query_grad: bfloat16 [8192, 512], P(('groups', 'qrow', 'kcol')), parts along dimension 0
- key_grad: bfloat16 [8192, 128], P(('groups', 'kcol', 'qrow')), parts along dimension 0
- value_grad: bfloat16 [8192, 128], P(('groups', 'kcol', 'qrow')), parts along dimension 0
There are 2 independent parts, one for each index of `groups`. A program takes and returns all parts, laid end to end along the dimension named above; each array names one. Nothing has to cross between parts.
Inputs may be any that keep to these rules, and one draw needn't show every extreme that they name: `pattern`: each row lists distinct key blocks, block b among them. Counting key blocks in aligned groups of 8, a row has at least one entry in every group, at most 4 in one group, and exactly 4 in the group that holds b.
All inputs are finite; a program needn't handle non-finite values.
Results may differ from a plain program's by a relative error of at most 0.038.
Values may be sent and summed in bfloat16 or wider, within the bound.
A program may use at most 128 MiB of HBM per device.

v0:
```python
import jax
import jax.numpy as jnp
from jax import lax
from jax.sharding import PartitionSpec as P

H = 4
HD = 128
BLK = 128
SLOTS = 4


def body(queries, keys, values, out_grad, pattern):
    scaling = HD ** (-0.5)
    q_panel, g_panel = (
        lax.all_gather(queries, "kcol", axis=0, tiled=True),
        lax.all_gather(out_grad, "kcol", axis=0, tiled=True),
    )
    k_panel, v_panel = (
        lax.all_gather(keys, "qrow", axis=0, tiled=True),
        lax.all_gather(values, "qrow", axis=0, tiled=True),
    )
    own_rows = queries.shape[0]
    query_blocks = q_panel.shape[0] // BLK
    key_blocks = k_panel.shape[0] // BLK
    slot_count = min(SLOTS, key_blocks)
    column = lax.axis_index("kcol")
    listed = lax.dynamic_slice_in_dim(
        pattern, lax.axis_index("qrow") * query_blocks, query_blocks, 0
    )
    entry_count = listed.shape[1]
    in_group = listed // key_blocks == column
    ranking = (
        jnp.where(in_group, 0, 1) * entry_count + jnp.arange(entry_count, dtype=jnp.int32)[None, :]
    )
    ordering = jnp.argsort(ranking, axis=1)[:, :slot_count]
    picked = jnp.take_along_axis(listed, ordering, axis=1)
    usable = jnp.take_along_axis(in_group, ordering, axis=1)
    located = jnp.where(usable, picked - column * key_blocks, 0)
    k_tiles = k_panel.reshape(key_blocks, BLK, HD)
    v_tiles = v_panel.reshape(key_blocks, BLK, HD)
    q_blocks = q_panel.reshape(query_blocks, BLK, H, HD)
    g_blocks = g_panel.reshape(query_blocks, BLK, H, HD)

    def slot_tiles(where_at):
        k_slots = k_tiles[where_at].reshape(slot_count * BLK, HD)
        v_slots = v_tiles[where_at].reshape(slot_count * BLK, HD)
        return (k_slots, v_slots)

    def scores_of(q_block, k_slots, usable_row):
        scores = (
            jnp.einsum("thd,sd->hts", q_block, k_slots, preferred_element_type=jnp.float32)
            * scaling
        )
        column_ok = jnp.repeat(usable_row, BLK)
        return jnp.where(column_ok[None, None, :], scores, -1e30)

    def local_top(packed):
        q_block, where_at, usable_row = packed
        k_slots, v_slots = slot_tiles(where_at)
        return jnp.max(scores_of(q_block, k_slots, usable_row), axis=2)

    local_max = lax.map(local_top, (q_blocks, located, usable))
    row_max = lax.pmax(local_max.astype(jnp.bfloat16), "kcol").astype(local_max.dtype)

    def forward(packed):
        q_block, where_at, usable_row, row_top = packed
        k_slots, v_slots = slot_tiles(where_at)
        weights = jnp.exp(scores_of(q_block, k_slots, usable_row) - row_top[:, :, None])
        totals = jnp.sum(weights, axis=2)
        mixture = jnp.einsum(
            "hts,sd->thd", weights.astype(jnp.bfloat16), v_slots, preferred_element_type=jnp.float32
        )
        return (mixture, totals)

    mixture, totals = lax.map(forward, (q_blocks, located, usable, row_max))
    part_out = mixture.reshape(query_blocks * BLK, H * HD)
    part_total = jnp.transpose(totals, (0, 2, 1)).reshape(query_blocks * BLK, H)
    panel_max = jnp.transpose(row_max, (0, 2, 1)).reshape(query_blocks * BLK, H)
    sum_out, sum_total = (
        lax.psum(part_out.astype(jnp.bfloat16), "kcol").astype(jnp.float32),
        lax.psum(part_total.astype(jnp.bfloat16), "kcol").astype(jnp.float32),
    )
    attended = (sum_out.reshape(-1, H, HD) / sum_total[:, :, None]).astype(jnp.bfloat16)
    log_sum = panel_max + jnp.log(sum_total)
    delta = jnp.sum(
        g_panel.reshape(-1, H, HD).astype(jnp.float32) * attended.astype(jnp.float32), axis=2
    )
    result = lax.dynamic_slice_in_dim(attended.reshape(-1, H * HD), column * own_rows, own_rows, 0)
    log_blocks = jnp.transpose(log_sum.reshape(query_blocks, BLK, H), (0, 2, 1))
    delta_blocks = jnp.transpose(delta.reshape(query_blocks, BLK, H), (0, 2, 1))

    def backward(carried, packed):
        key_acc, value_acc = carried
        q_block, g_block, where_at, usable_row, log_row, delta_row = packed
        k_slots, v_slots = slot_tiles(where_at)
        prob_full = jnp.exp(scores_of(q_block, k_slots, usable_row) - log_row[:, :, None])
        prob_low = prob_full.astype(jnp.bfloat16)
        grad_prob = jnp.einsum("thd,sd->hts", g_block, v_slots, preferred_element_type=jnp.float32)
        grad_score = (prob_full * (grad_prob - delta_row[:, :, None])).astype(jnp.bfloat16)
        grad_query = (
            jnp.einsum("hts,sd->thd", grad_score, k_slots, preferred_element_type=jnp.float32)
            * scaling
        )
        grad_key = (
            jnp.einsum("hts,thd->sd", grad_score, q_block, preferred_element_type=jnp.float32)
            * scaling
        )
        grad_value = jnp.einsum(
            "hts,thd->sd", prob_low, g_block, preferred_element_type=jnp.float32
        )
        key_acc = key_acc.at[where_at].add(grad_key.reshape(slot_count, BLK, HD))
        value_acc = value_acc.at[where_at].add(grad_value.reshape(slot_count, BLK, HD))
        return ((key_acc, value_acc), grad_query)

    empty_acc = jnp.zeros((key_blocks, BLK, HD), jnp.float32)
    (key_acc, value_acc), grad_queries = lax.scan(
        backward,
        (empty_acc, empty_acc),
        (q_blocks, g_blocks, located, usable, log_blocks, delta_blocks),
    )
    query_part = grad_queries.reshape(query_blocks * BLK, H * HD)
    grad_q = lax.psum_scatter(
        query_part.astype(jnp.bfloat16), "kcol", scatter_dimension=0, tiled=True
    )
    grad_k, grad_v = (
        lax.psum_scatter(
            key_acc.reshape(-1, HD).astype(jnp.bfloat16), "qrow", scatter_dimension=0, tiled=True
        ).astype(jnp.float32),
        lax.psum_scatter(
            value_acc.reshape(-1, HD).astype(jnp.bfloat16), "qrow", scatter_dimension=0, tiled=True
        ).astype(jnp.float32),
    )
    return (result, grad_q, grad_k.astype(jnp.bfloat16), grad_v.astype(jnp.bfloat16))


def solution(mesh):
    return jax.shard_map(
        body,
        mesh=mesh,
        in_specs=(
            P(("groups", "qrow", "kcol"), None),
            P(("groups", "kcol", "qrow"), None),
            P(("groups", "kcol", "qrow"), None),
            P(("groups", "qrow", "kcol"), None),
            P("groups", None),
        ),
        out_specs=(
            P(("groups", "qrow", "kcol"), None),
            P(("groups", "qrow", "kcol"), None),
            P(("groups", "kcol", "qrow"), None),
            P(("groups", "kcol", "qrow"), None),
        ),
        check_vma=False,
    )
```

profile of v0, /device:TPU:0, one launch (start us, length us, event | category | flops | bytes accessed | tf_op | source)
XLA Modules:
  0.0 303.4 jit_solution(11228385538093810854)
XLA Ops:
  12.4 7.2 %all_gather.13 = bf16[1024,128]{1,0:T(8,128)(2,1)S(1)} all-gather(bf16[256,128]{1,0:T(8,128)(2,1)S(1)} %copy-done.5), channel_id=1, replica_groups=mesh['groups'=2,'qrow'=4,'kcol'=4] {'qrow'}, dimensions={0}, use_global_device_ids=true | all-gather | bytes 327680 | tf_op jit(solution)/shard_map/all_gather | solution.py:19
  19.7 5.8 %all_gather.12 = bf16[1024,128]{1,0:T(8,128)(2,1)S(1)} all-gather(bf16[256,128]{1,0:T(8,128)(2,1)S(1)} %copy-done.6), channel_id=1, replica_groups=mesh['groups'=2,'qrow'=4,'kcol'=4] {'qrow'}, dimensions={0}, use_global_device_ids=true | all-gather | bytes 327680 | tf_op jit(solution)/shard_map/all_gather | solution.py:20
  25.5 14.7 %all-gather.3.cloned.1.call-done = bf16[1024,512]{1,0:T(8,128)(2,1)} async-done(((bf16[256,512]{1,0:T(8,128)(2,1)}), bf16[1024,512]{1,0:T(8,128)(2,1)}) %all-gather.3.cloned.1.call-update) | async-done | bytes 1048592 | tf_op jit(solution)/shard_map/all_gather | solution.py:15
  40.2 1.3 reshape.267
  41.8 8.5 %while.36 = (s32[]{:T(128)}, bf16[8,4,128]{2,1,0:T(4,128)(2,1)S(1)}, pred[8,4]{1,0:T(8,128)(4,1)S(1)}, s32[8,4]{1,0:T(8,128)S(1)}, bf16[8,128,128]{2,1,0:T(8,128...) while((s32[]{:T(128)}, bf16[8,4,128]{2,1,0:T(4,128)(2,1)S(1)}, pred[8,4]{1,0:T(8,128)(4,1)S(1)}, ...), condition=%wide.region_3.4_spmd, body=%wide.region_1.3_spmd.sunk | while | flops 67895824 | bytes 532649 | solution.py:62
  50.3 11.0 %pmax.7 = bf16[8,4,128]{2,1,0:T(4,128)(2,1)S(1)} all-reduce(bf16[8,4,128]{2,1,0:T(4,128)(2,1)S(1)} %get-tuple-element.150), channel_id=1, replica_groups=mesh['groups'=2,'qrow'=4,'kcol'=4] {'kcol'}, use_global_device_ids=true, to_apply=%region_4.5 | all-reduce | flops 4096 | bytes 16384 | tf_op jit(solution)/shard_map/pmax | solution.py:63
  61.5 16.7 %while.37 = (s32[]{:T(128)}, bf16[8,128,4,128]{1,3,2,0:T(8,128)(2,1)S(1)}, bf16[8,4,128]{2,1,0:T(4,128)(2,1)S(1)}, s32[8,4]{1,0:T(8,128)S(1)}, bf16[8,128,128]{2...) while((s32[]{:T(128)}, ...), condition=%wide.region_7.8_spmd, body=%wide.region_5.7_spmd.sunk | while | flops 135528976 | bytes 2242777 | solution.py:75
  78.2 1.4 copy.57
  79.7 2.4 copy.103
  82.2 8.9 %psum.15 = bf16[1024,4]{0,1:T(4,128)(2,1)S(1)} all-reduce(bf16[1024,4]{0,1:T(4,128)(2,1)S(1)} %bitcast.307), channel_id=1, replica_groups=mesh['groups'=2,'qrow'=4,'kcol'=4] {'kcol'}, use_global_device_ids=true, to_apply=%region_9.10 | all-reduce | flops 4096 | bytes 16384 | tf_op jit(solution)/shard_map/psum | solution.py:81
  91.3 1.9 reshape.184
  93.2 2.2 reshape.268
  95.3 36.9 %all-reduce.2.cloned.1.call-done = bf16[1024,512]{1,0:T(8,128)(2,1)} async-done(((bf16[1024,512]{1,0:T(8,128)(2,1)}), bf16[1024,512]{1,0:T(8,128)(2,1)}) %all-reduce.2.cloned.1.call-update) | async-done | bytes 1048592 | tf_op jit(solution)/shard_map/psum | solution.py:80
  132.3 2.7 reshape.182
  135.0 16.3 %multiply_reduce_fusion = f32[1024,4]{1,0:T(8,128)} fusion(f32[1024,4,128]{2,1,0:T(4,128)S(1)} %reshape.184, f32[1024,4,128]{2,1,0:T(4,128)} %reshape.182, f32[1024,4]{1,0:T(8,128)S(1)} %copy.58), kind=kLoop, calls=%fused_computation.81 | loop fusion | flops 2617344 | bytes 4227072 | tf_op jit(solution)/shard_map/reduce_sum | solution.py:85
  151.3 1.8 copy.66
  153.2 1.2 broadcast.120
  154.5 68.7 %while.38 = (s32[]{:T(128)}, f32[8,128,128]{2,1,0:T(8,128)S(1)}, f32[8,128,128]{2,1,0:T(8,128)S(1)}, bf16[8,128,4,128]{1,3,2,0:T(8,128)(2,1)}, s32[8,4]{1,0:T(8,...) while((s32[]{:T(128)}, f32[8,128,128]{2,1,0:T(8,128)S(1)}, ...), condition=%wide.region_14.15_spmd, body=%wide.region_11.14_spmd.sunk | while | flops 337904640 | bytes 8934213 | solution.py:116
  155.2 1.3 fusion.101
  157.1 1.0 constant_dynamic-slice_fusion.10
  160.0 1.2 fusion.103
  163.8 1.3 fusion.101
  165.7 1.0 constant_dynamic-slice_fusion.10
  168.6 1.2 fusion.103
  172.4 1.3 fusion.101
  174.3 1.0 constant_dynamic-slice_fusion.10
  177.2 1.2 fusion.103
  181.0 1.3 fusion.101
  182.9 1.0 constant_dynamic-slice_fusion.10
  185.8 1.2 fusion.103
  189.6 1.3 fusion.101
  191.5 1.0 constant_dynamic-slice_fusion.10
  194.4 1.2 fusion.103
  198.2 1.3 fusion.101
  200.1 1.0 constant_dynamic-slice_fusion.10
  203.0 1.2 fusion.103
  206.8 1.3 fusion.101
  208.7 1.0 constant_dynamic-slice_fusion.10
  211.6 1.2 fusion.103
  215.4 1.3 fusion.101
  217.3 1.0 constant_dynamic-slice_fusion.10
  220.2 1.2 fusion.103
  225.7 1.2 copy.102
  226.9 1.2 div.29
  228.3 1.1 copy-done.3
  230.5 13.1 %reduce-scatter.6.cloned.1.call-done = bf16[256,128]{1,0:T(8,128)(2,1)} async-done(((bf16[1024,128]{1,0:T(8,128)(2,1)}), bf16[256,128]{1,0:T(8,128)(2,1)}) %reduce-scatter.6.cloned.1.call-update) | async-done | bytes 65552 | tf_op jit(solution)/shard_map/reduce_scatter | solution.py:126
  243.6 22.9 %reduce-scatter.8.cloned.1.call-done = bf16[256,128]{1,0:T(8,128)(2,1)} async-done(((bf16[1024,128]{1,0:T(8,128)(2,1)}), bf16[256,128]{1,0:T(8,128)(2,1)}) %reduce-scatter.8.cloned.1.call-update) | async-done | bytes 65552 | tf_op jit(solution)/shard_map/reduce_scatter | solution.py:129
  266.6 30.0 %reduce-scatter.4.cloned.1.call-done = bf16[256,512]{1,0:T(8,128)(2,1)} async-done(((bf16[1024,512]{1,0:T(8,128)(2,1)}), bf16[256,512]{1,0:T(8,128)(2,1)}) %reduce-scatter.4.cloned.1.call-update) | async-done | bytes 262160 | tf_op jit(solution)/shard_map/reduce_scatter | solution.py:122
  (330 shorter events, 73.8 us)
Async XLA Ops:
  7.2 33.1 %all-gather.3.cloned.1.call-start = ((), (), s32[]{:S(2)}) async-start(), calls=%async_computation.3 | async-start | bytes 1310720 | tf_op jit(solution)/shard_map/all_gather | solution.py:15
  7.9 83.4 %all-gather.5.cloned.1.call-start = ((), (), s32[]{:S(2)}) async-start(), calls=%async_computation.5 | async-start | bytes 1310720 | tf_op jit(solution)/shard_map/all_gather | solution.py:16
  8.6 123.6 %all-reduce.2.cloned.1.call-start = ((), (), s32[]{:S(2)}) async-start(), calls=%async_computation.4 | async-start | bytes 2097152 | tf_op jit(solution)/shard_map/psum | solution.py:80
  11.3 1.1 copy-start.5
  11.4 8.3 %copy-start.6 = (bf16[256,128]{1,0:T(8,128)(2,1)S(1)}, bf16[256,128]{1,0:T(8,128)(2,1)}, u32[]{:S(2)}) copy-start(bf16[256,128]{1,0:T(8,128)(2,1)} %param.13) | copy-start | bytes 196612
  78.2 3.9 %copy-start = (bf16[8,128,4,128]{3,1,2,0:T(8,128)(2,1)}, bf16[8,128,4,128]{3,1,2,0:T(8,128)(2,1)S(1)}, u32[]{:S(2)}) copy-start(bf16[8,128,4,128]{3,1,2,0:T(8,128)(2,1)S(1)} %get-tuple-element.548) | copy-start | bytes 3145732
  82.1 161.5 %reduce-scatter.6.cloned.1.call-start = ((), (), s32[]{:S(2)}) async-start(), calls=%async_computation.7 | async-start | bytes 327680 | tf_op jit(solution)/shard_map/reduce_scatter | solution.py:126
  91.2 43.8 %copy-start.1 = (f32[1024,4]{1,0:T(8,128)}, f32[1024,4]{1,0:T(8,128)S(1)}, u32[]{:S(2)}) copy-start(f32[1024,4]{1,0:T(8,128)S(1)} %copy.58) | copy-start | bytes 49156
  154.5 0.7 copy-start.7
  159.1 3.9 %copy-start.8 = (f32[8,4,128]{2,0,1:T(8,128)S(1)}, f32[8,4,128]{2,0,1:T(8,128)}, u32[]{:S(2)}) copy-start(f32[8,4,128]{2,0,1:T(8,128)} %copy-done.7) | copy-start | bytes 49156 | tf_op jit(solution)/shard_map/while
  163.1 0.7 copy-start.7
  167.7 4.0 %copy-start.8 = (f32[8,4,128]{2,0,1:T(8,128)S(1)}, f32[8,4,128]{2,0,1:T(8,128)}, u32[]{:S(2)}) copy-start(f32[8,4,128]{2,0,1:T(8,128)} %copy-done.7) | copy-start | bytes 49156 | tf_op jit(solution)/shard_map/while
  171.7 0.7 copy-start.7
  176.3 4.0 %copy-start.8 = (f32[8,4,128]{2,0,1:T(8,128)S(1)}, f32[8,4,128]{2,0,1:T(8,128)}, u32[]{:S(2)}) copy-start(f32[8,4,128]{2,0,1:T(8,128)} %copy-done.7) | copy-start | bytes 49156 | tf_op jit(solution)/shard_map/while
  180.3 0.7 copy-start.7
  184.9 4.0 %copy-start.8 = (f32[8,4,128]{2,0,1:T(8,128)S(1)}, f32[8,4,128]{2,0,1:T(8,128)}, u32[]{:S(2)}) copy-start(f32[8,4,128]{2,0,1:T(8,128)} %copy-done.7) | copy-start | bytes 49156 | tf_op jit(solution)/shard_map/while
  188.9 0.7 copy-start.7
  193.5 4.0 %copy-start.8 = (f32[8,4,128]{2,0,1:T(8,128)S(1)}, f32[8,4,128]{2,0,1:T(8,128)}, u32[]{:S(2)}) copy-start(f32[8,4,128]{2,0,1:T(8,128)} %copy-done.7) | copy-start | bytes 49156 | tf_op jit(solution)/shard_map/while
  197.5 0.7 copy-start.7
  202.1 3.9 %copy-start.8 = (f32[8,4,128]{2,0,1:T(8,128)S(1)}, f32[8,4,128]{2,0,1:T(8,128)}, u32[]{:S(2)}) copy-start(f32[8,4,128]{2,0,1:T(8,128)} %copy-done.7) | copy-start | bytes 49156 | tf_op jit(solution)/shard_map/while
  206.0 0.7 copy-start.7
  210.7 4.0 %copy-start.8 = (f32[8,4,128]{2,0,1:T(8,128)S(1)}, f32[8,4,128]{2,0,1:T(8,128)}, u32[]{:S(2)}) copy-start(f32[8,4,128]{2,0,1:T(8,128)} %copy-done.7) | copy-start | bytes 49156 | tf_op jit(solution)/shard_map/while
  214.6 0.7 copy-start.7
  219.3 4.0 %copy-start.8 = (f32[8,4,128]{2,0,1:T(8,128)S(1)}, f32[8,4,128]{2,0,1:T(8,128)}, u32[]{:S(2)}) copy-start(f32[8,4,128]{2,0,1:T(8,128)} %copy-done.7) | copy-start | bytes 49156 | tf_op jit(solution)/shard_map/while
  223.2 1.7 copy-start.4
  224.0 42.5 %reduce-scatter.8.cloned.1.call-start = ((), (), s32[]{:S(2)}) async-start(), calls=%async_computation.8 | async-start | bytes 327680 | tf_op jit(solution)/shard_map/reduce_scatter | solution.py:129
  224.9 71.7 %reduce-scatter.4.cloned.1.call-start = ((), (), s32[]{:S(2)}) async-start(), calls=%async_computation.6 | async-start | bytes 1310720 | tf_op jit(solution)/shard_map/reduce_scatter | solution.py:122
  225.7 1.2 copy-start.2
  228.1 1.2 copy-start.3
Sparse Core Ops, SparseCore 0:
  9.6 30.6 all-gather.2
  41.8 28.0 all-gather.4
  82.3 49.9 all-reduce.1
  224.2 19.4 reduce-scatter.5
  246.5 20.0 reduce-scatter.7
  269.4 27.0 reduce-scatter.3
where the time goes:
time: 304 us; the launch traced here: 303 us
  waiting for transfers between devices  119 us (39%)
  local copies, waits for them, and re-layouts  60.9 us (20%)
  matrix products  40.9 us (13%)
  other arithmetic  32.9 us (11%)
  blocking collectives  32.9 us (11%)
  between operations  14.4 us (5%)
    psum x1, waiting for transfers between devices, body(): lax.psum(part_out.astype(jnp.bfloat16), 'kcol').astype(jnp.float32)  36.9 us
    reduce_scatter x1, waiting for transfers between devices, body(): lax.psum_scatter(query_part.astype(jnp.bfloat16), 'kcol', scatter_dimensi...  30 us
    reduce_scatter x1, waiting for transfers between devices, body(): lax.psum_scatter(value_acc.reshape(-1, HD).astype(jnp.bfloat16), 'qrow',...  22.9 us
    dot_general x24, matrix products, scores_of(): jnp.einsum('thd,sd->hts', q_block, k_slots, preferred_element_type=jnp.fl...  16.8 us
    reduce_sum x1, other arithmetic, body(): jnp.sum(g_panel.reshape(-1, H, HD).astype(jnp.float32) * attended.astype(...  16.3 us
    all_gather x1, waiting for transfers between devices, body(): lax.all_gather(queries, 'kcol', axis=0, tiled=True)  14.7 us
    gather x24, local copies, waits for them, and re-layouts, slot_tiles(): k_slots = k_tiles[where_at].reshape(slot_count * BLK, HD)  13.7 us
    reduce_scatter x1, waiting for transfers between devices, body(): lax.psum_scatter(key_acc.reshape(-1, HD).astype(jnp.bfloat16), 'qrow', sc...  13.1 us
  transfers between devices with their start and end apart: 6, of which 5 were waited for; matrix products, arithmetic and copies ran while one was open for 14% of the time, Pallas kernels for 0%

commit v1 on v0

v1 whole, which is shorter than its diff:
```python
import functools
import math

import jax
import jax.numpy as jnp
from jax import lax
from jax.experimental import pallas as pl
from jax.experimental.pallas import tpu as pltpu
from jax.sharding import PartitionSpec as P

H = 4
HD = 128
BLK = 128
MESH = pl.DeviceIdType.MESH
F32 = jnp.float32
BF16 = jnp.bfloat16


def dot(a, b):
    return jnp.dot(a, b, preferred_element_type=F32)


def dot_t(a, b):
    return lax.dot_general(a, b, (((0,), (0,)), ((), ())), preferred_element_type=F32)


def kernel(
    nq, nk, nnz, q_ref, g_ref, k_ref, v_ref, pat_ref, o_ref, dq_ref, dk_ref, dv_ref,
    kv, core_in, y_in, z_in, slots, s_scr, qs, gs, qt, gt, kc_scr, vc_scr, inv,
    ag_send, ag_recv, core_send, core_recv, y_send, y_recv, z_send, z_recv,
):
    ny = nq // 2
    qb = q_ref.shape[0] // BLK
    kb = k_ref.shape[0] // BLK
    key_blocks = nq * nk * kb
    chunk = 2 if nnz % 2 == 0 else 1
    scaling = HD ** (-0.5)
    r = lax.axis_index("qrow")
    c = lax.axis_index("kcol")
    y, core = r // 2, r % 2
    other = 1 - core

    def shard(c_at, y_at, core_at):
        return c_at * nq + y_at * 2 + core_at

    def zed(d):
        return (c + d) % nk

    def why(e):
        return (y + e) % ny

    def at(c_to, y_to, core_to):
        return {"qrow": y_to * 2 + core_to, "kcol": c_to}

    def remote(src, dst, send, recv, where):
        return pltpu.make_async_remote_copy(
            src_ref=src, dst_ref=dst, send_sem=send, recv_sem=recv,
            device_id=where, device_id_type=MESH,
        )

    core_peer = at(c, y, other)

    barrier = pltpu.get_barrier_semaphore()
    for d in range(1, nk):
        pl.semaphore_signal(barrier, inc=1, device_id=at(zed(d), y, core), device_id_type=MESH)
    for e in range(1, ny):
        pl.semaphore_signal(barrier, inc=1, device_id=at(c, why(e), core), device_id_type=MESH)
    pl.semaphore_signal(barrier, inc=1, device_id=core_peer, device_id_type=MESH)

    own = shard(c, y, core)
    kv[own, 0] = k_ref[...].reshape(kb, BLK, HD)
    kv[own, 1] = v_ref[...].reshape(kb, BLK, HD)
    pl.semaphore_wait(barrier, nk - 1 + ny - 1 + 1)

    z_sends = nk - 1
    y_sends = nk * (ny - 1)

    def gather(slot, s, where):
        return remote(kv.at[s], kv.at[s], ag_send.at[slot], ag_recv.at[s], where)

    def arrived(s):
        gather(0, s, core_peer).wait_recv()

    for d in range(1, nk):
        gather(d - 1, own, at(zed(d), y, core)).start()
    for e in range(1, ny):
        gather(z_sends + e - 1, own, at(c, why(e), core)).start()
    gather(z_sends + y_sends, own, core_peer).start()

    for b in range(qb):
        for h in range(H):
            q_h = q_ref[b * BLK : (b + 1) * BLK, h * HD : (h + 1) * HD]
            g_h = g_ref[b * BLK : (b + 1) * BLK, h * HD : (h + 1) * HD]
            qs[b, h * BLK : (h + 1) * BLK, :] = q_h
            gs[b, h * BLK : (h + 1) * BLK, :] = g_h
            qt[b, :, h * BLK : (h + 1) * BLK] = q_h.T
            gt[b, :, h * BLK : (h + 1) * BLK] = g_h.T

    zero_slot = qb * nnz
    slots[0, zero_slot] = jnp.zeros((BLK, HD), F32)
    slots[1, zero_slot] = jnp.zeros((BLK, HD), F32)
    first_row = (r * nk + c) * qb

    for d in range(1, nk):
        s = shard(zed(nk - d), y, core)
        arrived(s)
        for e in range(1, ny):
            gather(z_sends + d * (ny - 1) + e - 1, s, at(c, why(e), core)).start()
        gather(z_sends + y_sends + d, s, core_peer).start()

    def invert(j, carry):
        for b in range(qb):
            found = jnp.int32(zero_slot)
            for n in range(nnz):
                found = jnp.where(pat_ref[first_row + b, n] == j, b * nnz + n, found)
            inv[b, j] = found
        return carry

    lax.fori_loop(0, key_blocks, invert, 0)

    def from_y(i, carry):
        e, d = i // nk + 1, i % nk
        s = shard(zed(nk - d), why(ny - e), core)
        arrived(s)
        gather(z_sends + y_sends + nk + i, s, core_peer).start()
        return carry

    lax.fori_loop(0, y_sends, from_y, 0)

    def from_core(i, carry):
        arrived(shard(i % nk, i // nk, other))
        return carry

    lax.fori_loop(0, nk * ny, from_core, 0)

    rows = chunk * BLK
    for b in range(qb):
        for n in range(nnz):
            j = pat_ref[first_row + b, n]
            kc_scr[b, n * BLK : (n + 1) * BLK, :] = kv[j // kb, 0, j % kb]
            vc_scr[b, n * BLK : (n + 1) * BLK, :] = kv[j // kb, 1, j % kb]
    for b in range(qb):
        top = None
        for n in range(0, nnz, chunk):
            part = slice(n * BLK, n * BLK + rows)
            scores = dot(kc_scr[b, part, :], qt[b])
            s_scr[b, part, :] = scores
            high = jnp.max(scores, axis=0, keepdims=True)
            top = high if top is None else jnp.maximum(top, high)
        total = jnp.zeros((1, H * BLK), F32)
        mix = jnp.zeros((HD, H * BLK), F32)
        for n in range(0, nnz, chunk):
            part = slice(n * BLK, n * BLK + rows)
            weights = jnp.exp2((s_scr[b, part, :] - top) * (scaling * math.log2(math.e)))
            s_scr[b, part, :] = weights
            total = total + jnp.sum(weights, axis=0, keepdims=True)
            mix = mix + dot_t(vc_scr[b, part, :], weights.astype(BF16))
        attended = (mix / total).astype(BF16)
        delta = jnp.sum(gt[b].astype(F32) * attended.astype(F32), axis=0, keepdims=True)
        share = 1.0 / total
        for h in range(H):
            o_ref[b * BLK : (b + 1) * BLK, h * HD : (h + 1) * HD] = attended[
                :, h * BLK : (h + 1) * BLK
            ].T
        grad_q = jnp.zeros((HD, H * BLK), F32)
        for n in range(0, nnz, chunk):
            part = slice(n * BLK, n * BLK + rows)
            grad_prob = dot(vc_scr[b, part, :], gt[b])
            prob = s_scr[b, part, :] * share
            grad_score = (prob * (grad_prob - delta)).astype(BF16)
            grad_v = dot(prob.astype(BF16), gs[b])
            grad_k = dot(grad_score, qs[b]) * scaling
            grad_q = grad_q + dot_t(kc_scr[b, part, :], grad_score)
            for i in range(chunk):
                slots[0, b * nnz + n + i] = grad_k[i * BLK : (i + 1) * BLK]
                slots[1, b * nnz + n + i] = grad_v[i * BLK : (i + 1) * BLK]
        grad_q = (grad_q * scaling).astype(BF16)
        for h in range(H):
            dq_ref[b * BLK : (b + 1) * BLK, h * HD : (h + 1) * HD] = grad_q[
                :, h * BLK : (h + 1) * BLK
            ].T

    def gathers_sent(i, carry):
        gather(i, own, core_peer).wait_send()
        return carry

    lax.fori_loop(0, z_sends + y_sends + nk * ny, gathers_sent, 0)

    def partial(s, which, half):
        j = s * kb + half
        value = slots[which, inv[0, j]]
        for b in range(1, qb):
            value = value + slots[which, inv[b, j]]
        return value

    def to_core(i, s):
        return remote(kv.at[s], core_in.at[i], core_send.at[i], core_recv.at[i], core_peer)

    def to_y(i, s, c_at, where, slot):
        return remote(kv.at[s], y_in.at[i], y_send.at[slot], y_recv.at[i], where)

    def to_z(i, s, where):
        return remote(kv.at[s], z_in.at[i], z_send.at[i], z_recv.at[i], where)

    def order(i):
        return zed((i % nk + 1) % nk), why((i // nk + 1) % ny)

    def core_step(i, carry):
        c_at, y_at = order(i)
        s = shard(c_at, y_at, other)
        for which in range(2):
            for half in range(kb):
                kv[s, which, half] = partial(s, which, half).astype(BF16)
        to_core(i, s).start()
        return carry

    lax.fori_loop(0, nk * ny, core_step, 0)

    def y_step(i, carry):
        c_at, y_at = order(i)
        s = shard(c_at, y_at, core)
        to_core(i, s).wait_recv()
        for which in range(2):
            for half in range(kb):
                value = partial(s, which, half) + core_in[i, which, half].astype(F32)
                kv[s, which, half] = value.astype(BF16)
        to_y(i, s, c_at, at(c, y_at, core), i).start()
        return carry

    lax.fori_loop(0, y_sends, y_step, 0)

    def summed(d, s, which, half):
        i = y_sends + (d + nk - 1) % nk
        value = partial(s, which, half) + core_in[i, which, half].astype(F32)
        for e in range(1, ny):
            value = value + y_in[(e - 1) * nk + (d + nk - 1) % nk, which, half].astype(F32)
        return value

    def landed(d, s):
        to_core(y_sends + (d + nk - 1) % nk, s).wait_recv()
        for e in range(1, ny):
            to_y((e - 1) * nk + (d + nk - 1) % nk, s, c, core_peer, 0).wait_recv()

    for d in range(1, nk):
        s = shard(zed(d), y, core)
        landed(d, s)
        for which in range(2):
            for half in range(kb):
                kv[s, which, half] = summed(d, s, which, half).astype(BF16)
        to_z(d - 1, s, at(zed(d), y, core)).start()
    landed(0, own)
    for d in range(1, nk):
        to_z(d - 1, own, core_peer).wait_recv()
    for which, out in ((0, dk_ref), (1, dv_ref)):
        for half in range(kb):
            value = summed(0, own, which, half)
            for d in range(1, nk):
                value = value + z_in[d - 1, which, half].astype(F32)
            out[half * BLK : (half + 1) * BLK, :] = value.astype(BF16)

    def core_sent(i, carry):
        to_core(i, own).wait_send()
        return carry

    def y_sent(i, carry):
        to_y(0, own, c, core_peer, i).wait_send()
        return carry

    lax.fori_loop(0, nk * ny, core_sent, 0)
    lax.fori_loop(0, y_sends, y_sent, 0)
    for d in range(1, nk):
        to_z(d - 1, own, core_peer).wait_send()


def body(nq, nk, queries, keys, values, out_grad, pattern):
    nnz = pattern.shape[1]
    ny = nq // 2
    qb = queries.shape[0] // BLK
    kb = keys.shape[0] // BLK
    shards = nq * nk
    block = (2, kb, BLK, HD)
    y_sends = nk * (ny - 1)
    dma = pltpu.SemaphoreType.DMA
    vmem = pl.BlockSpec(memory_space=pltpu.VMEM)
    return pl.pallas_call(
        functools.partial(kernel, nq, nk, nnz),
        out_shape=(
            jax.ShapeDtypeStruct(queries.shape, BF16),
            jax.ShapeDtypeStruct(queries.shape, BF16),
            jax.ShapeDtypeStruct(keys.shape, BF16),
            jax.ShapeDtypeStruct(keys.shape, BF16),
        ),
        in_specs=[vmem] * 4 + [pl.BlockSpec(memory_space=pltpu.SMEM)],
        out_specs=(vmem,) * 4,
        scratch_shapes=[
            pltpu.VMEM((shards,) + block, BF16),
            pltpu.VMEM((nk * ny,) + block, BF16),
            pltpu.VMEM((max(y_sends, 1),) + block, BF16),
            pltpu.VMEM((max(nk - 1, 1),) + block, BF16),
            pltpu.VMEM((2, qb * nnz + 1, BLK, HD), F32),
            pltpu.VMEM((qb, nnz * BLK, H * BLK), F32),
            pltpu.VMEM((qb, H * BLK, HD), BF16),
            pltpu.VMEM((qb, H * BLK, HD), BF16),
            pltpu.VMEM((qb, HD, H * BLK), BF16),
            pltpu.VMEM((qb, HD, H * BLK), BF16),
            pltpu.VMEM((qb, nnz * BLK, HD), BF16),
            pltpu.VMEM((qb, nnz * BLK, HD), BF16),
            pltpu.SMEM((qb, shards * kb), jnp.int32),
            dma((nk - 1 + y_sends + nk * ny,)),
            dma((shards,)),
            dma((nk * ny,)),
            dma((nk * ny,)),
            dma((max(y_sends, 1),)),
            dma((max(y_sends, 1),)),
            dma((max(nk - 1, 1),)),
            dma((max(nk - 1, 1),)),
        ],
        compiler_params=pltpu.CompilerParams(
            collective_id=0, has_side_effects=True, vmem_limit_bytes=58 * 1024 * 1024
        ),
    )(queries, out_grad, keys, values, pattern)


def solution(mesh):
    return jax.shard_map(
        functools.partial(body, mesh.shape["qrow"], mesh.shape["kcol"]),
        mesh=mesh,
        in_specs=(
            P(("groups", "qrow", "kcol"), None),
            P(("groups", "kcol", "qrow"), None),
            P(("groups", "kcol", "qrow"), None),
            P(("groups", "qrow", "kcol"), None),
            P("groups", None),
        ),
        out_specs=(
            P(("groups", "qrow", "kcol"), None),
            P(("groups", "qrow", "kcol"), None),
            P(("groups", "kcol", "qrow"), None),
            P(("groups", "kcol", "qrow"), None),
        ),
        check_vma=False,
    )
```

time: 304 us -> 56 us (0.18)
  waiting for transfers between devices: 119 us -> 0 us
  local copies, waits for them, and re-layouts: 60.9 us -> 5.45 us
  Pallas kernels: 0 us -> 49.6 us
  matrix products: 40.9 us -> 0 us
  other arithmetic: 32.9 us -> 0 us
  blocking collectives: 32.9 us -> 0 us
  between operations: 14.4 us -> 0.65 us
    reduce_scatter x3 -> x0, waiting for transfers between devices: 66.1 us -> none  [the longest x1 30 us: body(): lax.psum_scatter(query_part.astype(jnp.bfloat16), 'kcol', scatter_dimensi...]
    pallas_call x0 -> x1, Pallas kernels: none -> 49.6 us  [body(): pl.pallas_call(functools.partial(kernel, nq, nk, nnz), out_shape=(jax.Sha...]
    dot_general x64 -> x0, matrix products: 40.9 us -> none  [the longest x24 16.8 us: scores_of(): jnp.einsum('thd,sd->hts', q_block, k_slots, preferred_element_type=jnp.fl...]
    psum x1 -> x0, waiting for transfers between devices: 36.9 us -> none  [body(): lax.psum(part_out.astype(jnp.bfloat16), 'kcol').astype(jnp.float32)]
    gather x48 -> x0, local copies, waits for them, and re-layouts: 24.9 us -> none  [the longest x24 13.7 us: slot_tiles(): k_slots = k_tiles[where_at].reshape(slot_count * BLK, HD)]
    reduce_sum x1 -> x0, other arithmetic: 16.3 us -> none  [body(): jnp.sum(g_panel.reshape(-1, H, HD).astype(jnp.float32) * attended.astype(...]
    all_gather x2 -> x0, waiting for transfers between devices: 14.7 us -> none  [the longest x1 14.7 us: body(): lax.all_gather(queries, 'kcol', axis=0, tiled=True)]
    all_gather x2 -> x0, blocking collectives: 13.1 us -> none  [the longest x1 7.21 us: body(): lax.all_gather(keys, 'qrow', axis=0, tiled=True)]
  transfers between devices with their start and end apart: 6 -> 0, of which waited for: 5 -> 0; matrix products, arithmetic and copies ran while one was open for 14% -> 0% of each run, Pallas kernels for 0% -> 0%
where the time goes in v1:
time: 56 us; the launch traced here: 55.7 us
  Pallas kernels  49.6 us (89%)
  local copies, waits for them, and re-layouts  5.45 us (10%)
  between operations  0.65 us (1%)
    pallas_call x1, Pallas kernels, body(): pl.pallas_call(functools.partial(kernel, nq, nk, nnz), out_shape=(jax.Sha...  49.6 us
    unnamed x11, local copies, waits for them, and re-layouts  5.45 us

profile of v1, /device:TPU:0, one launch (start us, length us, event | category | flops | bytes accessed | tf_op | source)
XLA Modules:
  0.0 55.7 jit_solution(1435090699598364742)
XLA Ops:
  0.6 1.4 %copy.9.pat_ref = s32[32,10]{1,0:T(8,128)} copy(s32[32,10]{0,1:T(8,128)} %param.9) | data formatting | bytes 2560 | tf_op args[4]
  2.0 49.6 %shard_map.84 = (bf16[256,512]{1,0:T(8,128)(2,1)}, bf16[256,512]{1,0:T(8,128)(2,1)}, bf16[256,128]{1,0:T(8,128)(2,1)}, bf16[256,128]{1,0:T(8,128)(2,1)}) custom-call(bf16[256,512]{1,0:T(8,128)(2,1)} %q_ref.1, bf16[256,512]{1,0:T(8,128)(2,1)} %g_ref.1, bf16[256,128]{1,0:T(8,128)(2,1)} %k_ref.1, bf16[256,128]{1,0:T(8,128)(2,1)} %v_ref.1, s32[32,10]{1,0:T(8,128)} %copy.9.pat_ref), custom_call_target="tpu_custom_call" | custom-call | tf_op jit(solution)/shard_map/pallas_call | solution.py:285
  51.7 0.0 copy-start
  51.7 1.7 %copy.14 = bf16[256,512]{1,0:T(8,128)(2,1)} copy(bf16[256,512]{1,0:T(8,128)(2,1)} %get-tuple-element.8) | data formatting | bytes 524288
  53.4 0.0 copy-done
  53.4 0.0 copy-start.2
  53.4 0.7 %copy.15 = bf16[256,512]{1,0:T(8,128)(2,1)} copy(bf16[256,512]{1,0:T(8,128)(2,1)S(1)} %copy-done) | data formatting | bytes 524288
  54.1 0.2 copy-done.2
  54.2 0.0 copy-start.1
  54.2 0.6 %copy.16 = bf16[256,128]{1,0:T(8,128)(2,1)} copy(bf16[256,128]{1,0:T(8,128)(2,1)S(1)} %copy-done.2) | data formatting | bytes 131072
  54.9 0.2 copy-done.1
  55.1 0.6 %copy.17 = bf16[256,128]{1,0:T(8,128)(2,1)} copy(bf16[256,128]{1,0:T(8,128)(2,1)S(1)} %copy-done.1) | data formatting | bytes 131072
Async XLA Ops:
  51.7 1.7 %copy-start = (bf16[256,512]{1,0:T(8,128)(2,1)S(1)}, bf16[256,512]{1,0:T(8,128)(2,1)}, u32[]{:S(2)}) copy-start(bf16[256,512]{1,0:T(8,128)(2,1)} %get-tuple-element.9) | copy-start | bytes 786436
  53.4 0.9 %copy-start.2 = (bf16[256,128]{1,0:T(8,128)(2,1)S(1)}, bf16[256,128]{1,0:T(8,128)(2,1)}, u32[]{:S(2)}) copy-start(bf16[256,128]{1,0:T(8,128)(2,1)} %get-tuple-element.10) | copy-start | bytes 196612
  54.2 0.9 %copy-start.1 = (bf16[256,128]{1,0:T(8,128)(2,1)S(1)}, bf16[256,128]{1,0:T(8,128)(2,1)}, u32[]{:S(2)}) copy-start(bf16[256,128]{1,0:T(8,128)(2,1)} %get-tuple-element.11) | copy-start | bytes 196612

commit v2 on v1

v2 whole, which is shorter than its diff:
```python
import functools
import math

import jax
import jax.numpy as jnp
from jax import lax
from jax.experimental import pallas as pl
from jax.experimental.pallas import tpu as pltpu
from jax.sharding import PartitionSpec as P

H = 4
HD = 128
BLK = 128
MESH = pl.DeviceIdType.MESH
F32 = jnp.float32
BF16 = jnp.bfloat16


def dot(a, b):
    return jnp.dot(a, b, preferred_element_type=F32)


def dot_t(a, b):
    return lax.dot_general(a, b, (((0,), (0,)), ((), ())), preferred_element_type=F32)


def kernel(
    nq, nk, nnz, q_hbm, g_hbm, k_hbm, v_hbm, pat_ref, o_ref, dq_ref, dk_ref, dv_ref,
    k_all, v_all, core_in, y_in, z_in, slots, s_scr, q_ref, g_ref, qs, gs, qt, gt, kc_scr, vc_scr, inv,
    load_sem, ag_send, ag_recv, core_send, core_recv, y_send, y_recv, z_send, z_recv,
):
    ny = nq // 2
    qb = q_ref.shape[0] // BLK
    kb = k_hbm.shape[0]
    key_blocks = nq * nk * kb
    chunk = 2 if nnz % 2 == 0 else 1
    rows = chunk * BLK
    scaling = HD ** (-0.5)
    r = lax.axis_index("qrow")
    c = lax.axis_index("kcol")
    y, core = r // 2, r % 2
    other = 1 - core
    KEY, VALUE = 0, 1
    kv = (k_all, v_all)

    loads = [
        pltpu.make_async_copy(src, dst, load_sem.at[i])
        for i, (src, dst) in enumerate(
            (
                (k_hbm, k_all.at[pl.ds((c * nq + r) * kb, kb)]),
                (v_hbm, v_all.at[pl.ds((c * nq + r) * kb, kb)]),
                (q_hbm, q_ref),
                (g_hbm, g_ref),
            )
        )
    ]
    for load in loads:
        load.start()

    def shard(c_at, y_at, core_at):
        return c_at * nq + y_at * 2 + core_at

    def why(e):
        return (y + e) % ny

    def at(c_to, y_to, core_to):
        return {"qrow": y_to * 2 + core_to, "kcol": c_to}

    def held(w, s):
        return kv[w].at[pl.ds(s * kb, kb)]

    def remote(src, dst, send, recv, where):
        return pltpu.make_async_remote_copy(
            src_ref=src, dst_ref=dst, send_sem=send, recv_sem=recv,
            device_id=where, device_id_type=MESH,
        )

    core_peer = at(c, y, other)
    has_left, has_right = c > 0, c < nk - 1
    left, right = at(c - 1, y, core), at(c + 1, y, core)
    own = shard(c, y, core)
    barrier = pltpu.get_barrier_semaphore()

    def greet(where):
        pl.semaphore_signal(barrier, inc=1, device_id=where, device_id_type=MESH)

    pl.when(has_left)(lambda: greet(left))
    pl.when(has_right)(lambda: greet(right))
    for e in range(1, ny):
        greet(at(c, why(e), core))
    greet(core_peer)
    loads[0].wait()
    loads[1].wait()
    line_peers = (c + nk - 1) // nk + (2 * nk - 2 - c) // nk
    pl.semaphore_wait(barrier, line_peers + ny)

    y_sends = nk * (ny - 1)
    y_base = 2 * nk
    core_base = y_base + y_sends

    def gather(w, slot, s, where):
        return remote(held(w, s), held(w, s), ag_send.at[w, slot], ag_recv.at[w, s], where)

    def arrived(w, s):
        gather(w, 0, s, core_peer).wait_recv()

    def go_right(w, c_at):
        pl.when(has_right)(lambda: gather(w, c_at, shard(c_at, y, core), right).start())

    def go_left(w, c_at):
        pl.when(has_left)(lambda: gather(w, nk + c_at, shard(c_at, y, core), left).start())

    def go_y(w, c_at):
        for e in range(1, ny):
            slot = y_base + (e - 1) * nk + c_at
            gather(w, slot, shard(c_at, y, core), at(c, why(e), core)).start()

    def go_core(w, c_at, y_at):
        gather(w, core_base + y_at * nk + c_at, shard(c_at, y_at, core), core_peer).start()

    def along_z(w, i):
        @pl.when(c - i >= 0)
        def _():
            arrived(w, shard(c - i, y, core))
            go_right(w, c - i)
            go_y(w, c - i)
            go_core(w, c - i, y)

        @pl.when(c + i < nk)
        def _():
            arrived(w, shard(c + i, y, core))
            go_left(w, c + i)
            go_y(w, c + i)
            go_core(w, c + i, y)

    def along_y(w, i):
        def take(c_at, e):
            arrived(w, shard(c_at, why(e), core))
            go_core(w, c_at, why(e))

        def each(e, carry):
            pl.when(c - i >= 0)(lambda: take(c - i, e))
            if i:
                pl.when(c + i < nk)(lambda: take(c + i, e))
            return carry

        lax.fori_loop(1, ny, each, 0)

    def from_core(w):
        def each(i, carry):
            arrived(w, shard(i % nk, i // nk, other))
            return carry

        lax.fori_loop(0, nk * ny, each, 0)

    def gathers_sent(w):
        def each(c_at, carry):
            pl.when(has_right & (c_at <= c))(lambda: gather(w, c_at, own, right).wait_send())
            pl.when(has_left & (c_at >= c))(lambda: gather(w, nk + c_at, own, left).wait_send())
            return carry

        def rest(i, carry):
            gather(w, y_base + i, own, core_peer).wait_send()
            return carry

        lax.fori_loop(0, nk, each, 0)
        lax.fori_loop(0, y_sends + nk * ny, rest, 0)

    first_row = (r * nk + c) * qb
    zero_slot = qb * nnz
    parts = [slice(n * BLK, n * BLK + rows) for n in range(0, nnz, chunk)]

    def prepare():
        loads[2].wait()
        loads[3].wait()
        for b in range(qb):
            for h in range(H):
                q_h = q_ref[b * BLK : (b + 1) * BLK, h * HD : (h + 1) * HD]
                g_h = g_ref[b * BLK : (b + 1) * BLK, h * HD : (h + 1) * HD]
                qs[b, h * BLK : (h + 1) * BLK, :] = q_h
                gs[b, h * BLK : (h + 1) * BLK, :] = g_h
                qt[b, :, h * BLK : (h + 1) * BLK] = q_h.T
                gt[b, :, h * BLK : (h + 1) * BLK] = g_h.T
        slots[KEY, zero_slot] = jnp.zeros((BLK, HD), F32)
        slots[VALUE, zero_slot] = jnp.zeros((BLK, HD), F32)
        nothing = jnp.zeros(z_in.shape[2:], BF16)

        @pl.when(c == 0)
        def _():
            for w in range(2):
                z_in[w, 0] = nothing

        @pl.when(c == nk - 1)
        def _():
            for w in range(2):
                z_in[w, 1] = nothing

    def invert(j, carry):
        for b in range(qb):
            found = jnp.int32(zero_slot)
            for n in range(nnz):
                found = jnp.where(pat_ref[n, first_row + b] == j, b * nnz + n, found)
            inv[b, j] = found
        return carry

    def pick(w, scr, b):
        for n in range(nnz):
            scr[b, n * BLK : (n + 1) * BLK, :] = kv[w][pat_ref[n, first_row + b]]

    def score(b):
        pick(KEY, kc_scr, b)
        top = None
        for part in parts:
            scores = dot(kc_scr[b, part, :], qt[b])
            s_scr[b, part, :] = scores
            high = jnp.max(scores, axis=0, keepdims=True)
            top = high if top is None else jnp.maximum(top, high)
        return top

    def forward(b, top):
        total = jnp.zeros((1, H * BLK), F32)
        mix = jnp.zeros((HD, H * BLK), F32)
        for part in parts:
            weights = jnp.exp2((s_scr[b, part, :] - top) * (scaling * math.log2(math.e)))
            s_scr[b, part, :] = weights
            total = total + jnp.sum(weights, axis=0, keepdims=True)
            mix = mix + dot_t(vc_scr[b, part, :], weights.astype(BF16))
        attended = (mix / total).astype(BF16)
        delta = jnp.sum(gt[b].astype(F32) * attended.astype(F32), axis=0, keepdims=True)
        share = 1.0 / total
        for h in range(H):
            o_ref[b * BLK : (b + 1) * BLK, h * HD : (h + 1) * HD] = attended[
                :, h * BLK : (h + 1) * BLK
            ].T
        for n, part in enumerate(parts):
            prob = s_scr[b, part, :] * share
            s_scr[b, part, :] = prob
            grad_v = dot(prob.astype(BF16), gs[b])
            for i in range(chunk):
                slots[VALUE, b * nnz + n * chunk + i] = grad_v[i * BLK : (i + 1) * BLK]
        return delta

    def backward(b, delta):
        grad_q = jnp.zeros((HD, H * BLK), F32)
        for n, part in enumerate(parts):
            grad_prob = dot(vc_scr[b, part, :], gt[b])
            grad_score = (s_scr[b, part, :] * (grad_prob - delta)).astype(BF16)
            grad_k = dot(grad_score, qs[b]) * scaling
            grad_q = grad_q + dot_t(kc_scr[b, part, :], grad_score)
            for i in range(chunk):
                slots[KEY, b * nnz + n * chunk + i] = grad_k[i * BLK : (i + 1) * BLK]
        grad_q = (grad_q * scaling).astype(BF16)
        for h in range(H):
            dq_ref[b * BLK : (b + 1) * BLK, h * HD : (h + 1) * HD] = grad_q[
                :, h * BLK : (h + 1) * BLK
            ].T

    def partial(w, s, half):
        j = s * kb + half
        value = slots[w, inv[0, j]]
        for b in range(1, qb):
            value = value + slots[w, inv[b, j]]
        return value

    def to_core(w, i, s):
        return remote(
            held(w, s), core_in.at[w, i], core_send.at[w, i], core_recv.at[w, i], core_peer
        )

    def to_y(w, i, s, where):
        return remote(held(w, s), y_in.at[w, i], y_send.at[w, i], y_recv.at[w, i], where)

    def to_z(w, side, i, s, where):
        return remote(
            held(w, s), z_in.at[w, side, i], z_send.at[w, side, i], z_recv.at[w, side, i], where
        )

    def core_stage(w):
        def each(i, carry):
            c_at, y_at = (c + nk // 2 + i) % nk, (y + 1 + i // nk) % ny
            s = shard(c_at, y_at, other)
            for half in range(kb):
                kv[w][s * kb + half] = partial(w, s, half).astype(BF16)
            to_core(w, y_at * nk + c_at, s).start()
            return carry

        lax.fori_loop(0, nk * ny, each, 0)

    def y_stage(w):
        def one(c_at, e):
            y_at = why(e)
            s = shard(c_at, y_at, core)
            i = y_at * nk + c_at
            to_core(w, i, s).wait_recv()
            for half in range(kb):
                value = partial(w, s, half) + core_in[w, i, half].astype(F32)
                kv[w][s * kb + half] = value.astype(BF16)
            to_y(w, (e - 1) * nk + c_at, s, at(c, y_at, core)).start()

        def each(e, carry):
            for i in range(nk - 1, 0, -1):
                pl.when(c + i < nk)(lambda i=i: one(c + i, e))
                pl.when(c - i >= 0)(lambda i=i: one(c - i, e))
            one(c, e)
            return carry

        lax.fori_loop(1, ny, each, 0)

    def landed(w, c_at):
        to_core(w, y * nk + c_at, own).wait_recv()
        for e in range(1, ny):
            to_y(w, (e - 1) * nk + c_at, own, core_peer).wait_recv()

    def summed(w, c_at, half):
        value = partial(w, shard(c_at, y, core), half)
        value = value + core_in[w, y * nk + c_at, half].astype(F32)
        for e in range(1, ny):
            value = value + y_in[w, (e - 1) * nk + c_at, half].astype(F32)
        return value

    def z_stage(w):
        def one(c_at, side, has_source, where):
            landed(w, c_at)
            s = shard(c_at, y, core)
            pl.when(has_source)(lambda: to_z(w, side, c_at, own, where).wait_recv())
            for half in range(kb):
                value = summed(w, c_at, half) + z_in[w, side, c_at, half].astype(F32)
                kv[w][s * kb + half] = value.astype(BF16)
            to_z(w, side, c_at, s, where).start()

        for i in range(nk - 1, 0, -1):
            pl.when(c + i < nk)(lambda i=i: one(c + i, 0, has_left, right))
            pl.when(c - i >= 0)(lambda i=i: one(c - i, 1, has_right, left))

    def finish(w, out):
        landed(w, c)
        pl.when(has_left)(lambda: to_z(w, 0, c, own, core_peer).wait_recv())
        pl.when(has_right)(lambda: to_z(w, 1, c, own, core_peer).wait_recv())
        for half in range(kb):
            value = summed(w, c, half)
            for side in range(2):
                value = value + z_in[w, side, c, half].astype(F32)
            out[half] = value.astype(BF16)

    def sums_sent(w):
        def core_sent(i, carry):
            to_core(w, i, own).wait_send()
            return carry

        def y_sent(i, carry):
            to_y(w, i, own, core_peer).wait_send()
            return carry

        def z_sent(i, carry):
            pl.when(i > c)(lambda: to_z(w, 0, i, own, core_peer).wait_send())
            pl.when(i < c)(lambda: to_z(w, 1, i, own, core_peer).wait_send())
            return carry

        lax.fori_loop(0, nk * ny, core_sent, 0)
        lax.fori_loop(0, y_sends, y_sent, 0)
        lax.fori_loop(0, nk, z_sent, 0)

    go_right(KEY, c)
    go_left(KEY, c)
    go_y(KEY, c)
    go_y(VALUE, c)
    go_core(KEY, c, y)
    go_core(VALUE, c, y)
    prepare()
    for i in range(1, nk):
        along_z(KEY, i)
        if i == 1:
            go_right(VALUE, c)
            go_left(VALUE, c)
            lax.fori_loop(0, key_blocks, invert, 0)
        along_y(KEY, i - 1)
        if i > 1:
            along_z(VALUE, i - 1)
        if i > 2:
            along_y(VALUE, i - 3)
    along_y(KEY, nk - 1)
    along_z(VALUE, nk - 1)
    for i in range(max(nk - 3, 0), nk - 1):
        along_y(VALUE, i)
    from_core(KEY)
    tops = [score(b) for b in range(qb)]
    along_y(VALUE, nk - 1)
    from_core(VALUE)
    for b in range(qb):
        pick(VALUE, vc_scr, b)
    deltas = [forward(b, tops[b]) for b in range(qb)]
    gathers_sent(VALUE)
    core_stage(VALUE)
    backward(0, deltas[0])
    y_stage(VALUE)
    for b in range(1, qb):
        backward(b, deltas[b])
    gathers_sent(KEY)
    core_stage(KEY)
    z_stage(VALUE)
    y_stage(KEY)
    finish(VALUE, dv_ref)
    z_stage(KEY)
    finish(KEY, dk_ref)
    sums_sent(VALUE)
    sums_sent(KEY)


def vmem_bytes(scratch, blocks):
    held = sum(
        math.prod(piece.shape) * jnp.dtype(piece.dtype).itemsize
        for piece in scratch
        if piece.dtype in (F32, BF16)
    )
    return min(held + 2 * blocks + (4 << 20), 60 << 20)


def body(nq, nk, queries, keys, values, out_grad, pattern):
    nnz = pattern.shape[1]
    ny = nq // 2
    qb = queries.shape[0] // BLK
    kb = keys.shape[0] // BLK
    shards = nq * nk
    block = (kb, BLK, HD)
    y_sends = nk * (ny - 1)
    dma = pltpu.SemaphoreType.DMA
    vmem = pl.BlockSpec(memory_space=pltpu.VMEM)
    hbm = pl.BlockSpec(memory_space=pltpu.HBM)
    scratch = [
        pltpu.VMEM((shards * kb, BLK, HD), BF16),
        pltpu.VMEM((shards * kb, BLK, HD), BF16),
        pltpu.VMEM((2, nk * ny) + block, BF16),
        pltpu.VMEM((2, max(y_sends, 1)) + block, BF16),
        pltpu.VMEM((2, 2, nk) + block, BF16),
        pltpu.VMEM((2, qb * nnz + 1, BLK, HD), F32),
        pltpu.VMEM((qb, nnz * BLK, H * BLK), F32),
        pltpu.VMEM(queries.shape, BF16),
        pltpu.VMEM(queries.shape, BF16),
        pltpu.VMEM((qb, H * BLK, HD), BF16),
        pltpu.VMEM((qb, H * BLK, HD), BF16),
        pltpu.VMEM((qb, HD, H * BLK), BF16),
        pltpu.VMEM((qb, HD, H * BLK), BF16),
        pltpu.VMEM((qb, nnz * BLK, HD), BF16),
        pltpu.VMEM((qb, nnz * BLK, HD), BF16),
        pltpu.SMEM((qb, shards * kb), jnp.int32),
        dma((4,)),
        dma((2, 2 * nk + y_sends + nk * ny)),
        dma((2, shards)),
        dma((2, nk * ny)),
        dma((2, nk * ny)),
        dma((2, max(y_sends, 1))),
        dma((2, max(y_sends, 1))),
        dma((2, 2, nk)),
        dma((2, 2, nk)),
    ]
    attended, grad_q, grad_k, grad_v = pl.pallas_call(
        functools.partial(kernel, nq, nk, nnz),
        out_shape=(
            jax.ShapeDtypeStruct(queries.shape, BF16),
            jax.ShapeDtypeStruct(queries.shape, BF16),
            jax.ShapeDtypeStruct(block, BF16),
            jax.ShapeDtypeStruct(block, BF16),
        ),
        in_specs=[hbm] * 4 + [pl.BlockSpec(memory_space=pltpu.SMEM)],
        out_specs=(vmem,) * 4,
        scratch_shapes=scratch,
        compiler_params=pltpu.CompilerParams(
            collective_id=0,
            has_side_effects=True,
            vmem_limit_bytes=vmem_bytes(scratch, 4 * (queries.size + keys.size)),
        ),
    )(queries, out_grad, keys.reshape(block), values.reshape(block), pattern.T)
    return attended, grad_q, grad_k.reshape(keys.shape), grad_v.reshape(keys.shape)


def solution(mesh):
    return jax.shard_map(
        functools.partial(body, mesh.shape["qrow"], mesh.shape["kcol"]),
        mesh=mesh,
        in_specs=(
            P(("groups", "qrow", "kcol"), None),
            P(("groups", "kcol", "qrow"), None),
            P(("groups", "kcol", "qrow"), None),
            P(("groups", "qrow", "kcol"), None),
            P("groups", None),
        ),
        out_specs=(
            P(("groups", "qrow", "kcol"), None),
            P(("groups", "qrow", "kcol"), None),
            P(("groups", "kcol", "qrow"), None),
            P(("groups", "kcol", "qrow"), None),
        ),
        check_vma=False,
    )
```

time: 56 us -> 61.4 us (1.096)
  Pallas kernels: 49.6 us -> 53.5 us
  local copies, waits for them, and re-layouts: 5.45 us -> 6.93 us
    pallas_call x1, Pallas kernels: 49.6 us -> 53.5 us  [body(): pl.pallas_call(functools.partial(kernel, nq, nk, nnz), out_shape=(jax.Sha...]
    unnamed x11 -> x14, local copies, waits for them, and re-layouts: 5.45 us -> 6.93 us
where the time goes in v2:
time: 61.4 us; the launch traced here: 61 us
  Pallas kernels  53.5 us (87%)
  local copies, waits for them, and re-layouts  6.93 us (11%)
  between operations  0.65 us (1%)
    pallas_call x1, Pallas kernels, body(): pl.pallas_call(functools.partial(kernel, nq, nk, nnz), out_shape=(jax.Sha...  53.5 us
    unnamed x14, local copies, waits for them, and re-layouts  6.93 us

profile of v2, /device:TPU:0, one launch (start us, length us, event | category | flops | bytes accessed | tf_op | source)
XLA Modules:
  0.0 61.0 jit_solution(8581901190351975021)
XLA Ops:
  0.6 0.0 copy-start
  0.6 0.9 %copy-done = bf16[256,512]{1,0:T(8,128)(2,1)S(1)} copy-done((bf16[256,512]{1,0:T(8,128)(2,1)S(1)}, bf16[256,512]{1,0:T(8,128)(2,1)}, u32[]{:S(2)}) %copy-start) | copy-done | bytes 262168
  1.6 0.0 copy-start.1
  1.6 0.9 %copy-done.1 = bf16[256,512]{1,0:T(8,128)(2,1)S(1)} copy-done((bf16[256,512]{1,0:T(8,128)(2,1)S(1)}, bf16[256,512]{1,0:T(8,128)(2,1)}, u32[]{:S(2)}) %copy-start.1) | copy-done | bytes 262168
  2.5 0.0 copy-start.2
  2.5 0.8 %copy-done.2 = bf16[256,128]{1,0:T(8,128)(2,1)S(1)} copy-done((bf16[256,128]{1,0:T(8,128)(2,1)S(1)}, bf16[256,128]{1,0:T(8,128)(2,1)}, u32[]{:S(2)}) %copy-start.2) | copy-done | bytes 65560
  3.4 0.0 copy-start.3
  3.4 0.8 %copy-done.3 = bf16[256,128]{1,0:T(8,128)(2,1)S(1)} copy-done((bf16[256,128]{1,0:T(8,128)(2,1)S(1)}, bf16[256,128]{1,0:T(8,128)(2,1)}, u32[]{:S(2)}) %copy-start.3) | copy-done | bytes 65560
  4.2 0.0 copy-start.4
  4.2 0.7 %copy-done.4 = s32[32,10]{0,1:T(8,128)S(1)} copy-done((s32[32,10]{0,1:T(8,128)S(1)}, s32[32,10]{0,1:T(8,128)}, u32[]{:S(2)}) %copy-start.4) | copy-done | bytes 1304
  4.9 53.5 %shard_map.84 = (bf16[256,512]{1,0:T(8,128)(2,1)S(1)}, bf16[256,512]{1,0:T(8,128)(2,1)S(1)}, bf16[2,128,128]{2,1,0:T(8,128)(2,1)S(1)}, bf16[2,128,128]{2,1,0:T(8,128)(2,1)S(1)}) custom-call(bf16[256,512]{1,0:T(8,128)(2,1)S(1)} %copy-done, bf16[256,512]{1,0:T(8,128)(2,1)S(1)} %copy-done.1, bf16[2,128,128]{2,1,0:T(8,128)(2,1)S(1)} %bitcast.7, ...), custom_call_target="tpu_custom_call" | custom-call | tf_op jit(solution)/shard_map/pallas_call | solution.py:456
  58.4 0.7 %copy.13 = bf16[256,512]{1,0:T(8,128)(2,1)} copy(bf16[256,512]{1,0:T(8,128)(2,1)S(1)} %get-tuple-element.16) | data formatting | bytes 524288
  59.1 0.7 %copy.14 = bf16[256,512]{1,0:T(8,128)(2,1)} copy(bf16[256,512]{1,0:T(8,128)(2,1)S(1)} %get-tuple-element.17) | data formatting | bytes 524288
  59.8 0.6 %copy.15 = bf16[256,128]{1,0:T(8,128)(2,1)} copy(bf16[256,128]{1,0:T(8,128)(2,1)S(1)} %bitcast.6) | data formatting | bytes 131072
  60.4 0.6 %copy.16 = bf16[256,128]{1,0:T(8,128)(2,1)} copy(bf16[256,128]{1,0:T(8,128)(2,1)S(1)} %bitcast.5) | data formatting | bytes 131072
Async XLA Ops:
  0.6 1.0 %copy-start = (bf16[256,512]{1,0:T(8,128)(2,1)S(1)}, bf16[256,512]{1,0:T(8,128)(2,1)}, u32[]{:S(2)}) copy-start(bf16[256,512]{1,0:T(8,128)(2,1)} %q_hbm.1) | copy-start | bytes 786436
  1.6 0.9 %copy-start.1 = (bf16[256,512]{1,0:T(8,128)(2,1)S(1)}, bf16[256,512]{1,0:T(8,128)(2,1)}, u32[]{:S(2)}) copy-start(bf16[256,512]{1,0:T(8,128)(2,1)} %g_hbm.1) | copy-start | bytes 786436
  2.5 0.8 %copy-start.2 = (bf16[256,128]{1,0:T(8,128)(2,1)S(1)}, bf16[256,128]{1,0:T(8,128)(2,1)}, u32[]{:S(2)}) copy-start(bf16[256,128]{1,0:T(8,128)(2,1)} %param.6) | copy-start | bytes 196612
  3.4 0.8 %copy-start.3 = (bf16[256,128]{1,0:T(8,128)(2,1)S(1)}, bf16[256,128]{1,0:T(8,128)(2,1)}, u32[]{:S(2)}) copy-start(bf16[256,128]{1,0:T(8,128)(2,1)} %param.7) | copy-start | bytes 196612
  4.2 0.7 %copy-start.4 = (s32[32,10]{0,1:T(8,128)S(1)}, s32[32,10]{0,1:T(8,128)}, u32[]{:S(2)}) copy-start(s32[32,10]{0,1:T(8,128)} %param.9) | copy-start | bytes 3844

commit v3 on v1

--- a/solution.py
+++ b/solution.py
@@ -25,13 +25,13 @@
 
 
 def kernel(
-    nq, nk, nnz, q_ref, g_ref, k_ref, v_ref, pat_ref, o_ref, dq_ref, dk_ref, dv_ref,
-    kv, core_in, y_in, z_in, slots, s_scr, qs, gs, qt, gt, kc_scr, vc_scr, inv,
+    nq, nk, nnz, q_hbm, g_hbm, k_hbm, v_hbm, pat_ref, o_ref, dq_ref, dk_ref, dv_ref,
+    q_ref, g_ref, load_sem, kv, core_in, y_in, z_in, slots, s_scr, qs, gs, qt, gt, kc_scr, vc_scr, inv,
     ag_send, ag_recv, core_send, core_recv, y_send, y_recv, z_send, z_recv,
 ):
     ny = nq // 2
     qb = q_ref.shape[0] // BLK
-    kb = k_ref.shape[0] // BLK
+    kb = k_hbm.shape[0]
     key_blocks = nq * nk * kb
     chunk = 2 if nnz % 2 == 0 else 1
     scaling = HD ** (-0.5)
@@ -59,6 +59,15 @@
         )
 
     core_peer = at(c, y, other)
+    own = shard(c, y, core)
+    loads = [
+        pltpu.make_async_copy(src, dst, load_sem.at[i])
+        for i, (src, dst) in enumerate(
+            ((k_hbm, kv.at[own, 0]), (v_hbm, kv.at[own, 1]), (q_hbm, q_ref), (g_hbm, g_ref))
+        )
+    ]
+    for load in loads:
+        load.start()
 
     barrier = pltpu.get_barrier_semaphore()
     for d in range(1, nk):
@@ -67,9 +76,8 @@
         pl.semaphore_signal(barrier, inc=1, device_id=at(c, why(e), core), device_id_type=MESH)
     pl.semaphore_signal(barrier, inc=1, device_id=core_peer, device_id_type=MESH)
 
-    own = shard(c, y, core)
-    kv[own, 0] = k_ref[...].reshape(kb, BLK, HD)
-    kv[own, 1] = v_ref[...].reshape(kb, BLK, HD)
+    loads[0].wait()
+    loads[1].wait()
     pl.semaphore_wait(barrier, nk - 1 + ny - 1 + 1)
 
     z_sends = nk - 1
@@ -87,6 +95,8 @@
         gather(z_sends + e - 1, own, at(c, why(e), core)).start()
     gather(z_sends + y_sends, own, core_peer).start()
 
+    loads[2].wait()
+    loads[3].wait()
     for b in range(qb):
         for h in range(H):
             q_h = q_ref[b * BLK : (b + 1) * BLK, h * HD : (h + 1) * HD]
@@ -112,7 +122,7 @@
         for b in range(qb):
             found = jnp.int32(zero_slot)
             for n in range(nnz):
-                found = jnp.where(pat_ref[first_row + b, n] == j, b * nnz + n, found)
+                found = jnp.where(pat_ref[n, first_row + b] == j, b * nnz + n, found)
             inv[b, j] = found
         return carry
 
@@ -136,7 +146,7 @@
     rows = chunk * BLK
     for b in range(qb):
         for n in range(nnz):
-            j = pat_ref[first_row + b, n]
+            j = pat_ref[n, first_row + b]
             kc_scr[b, n * BLK : (n + 1) * BLK, :] = kv[j // kb, 0, j % kb]
             vc_scr[b, n * BLK : (n + 1) * BLK, :] = kv[j // kb, 1, j % kb]
     for b in range(qb):
@@ -256,7 +266,7 @@
             value = summed(0, own, which, half)
             for d in range(1, nk):
                 value = value + z_in[d - 1, which, half].astype(F32)
-            out[half * BLK : (half + 1) * BLK, :] = value.astype(BF16)
+            out[half] = value.astype(BF16)
 
     def core_sent(i, carry):
         to_core(i, own).wait_send()
@@ -270,6 +280,15 @@
     lax.fori_loop(0, y_sends, y_sent, 0)
     for d in range(1, nk):
         to_z(d - 1, own, core_peer).wait_send()
+
+
+def vmem_bytes(scratch, blocks):
+    held = sum(
+        math.prod(piece.shape) * jnp.dtype(piece.dtype).itemsize
+        for piece in scratch
+        if piece.dtype in (F32, BF16)
+    )
+    return min(held + 2 * blocks + (4 << 20), 60 << 20)
 
 
 def body(nq, nk, queries, keys, values, out_grad, pattern):
@@ -279,46 +298,52 @@
     kb = keys.shape[0] // BLK
     shards = nq * nk
     block = (2, kb, BLK, HD)
+    tiles = (kb, BLK, HD)
     y_sends = nk * (ny - 1)
     dma = pltpu.SemaphoreType.DMA
     vmem = pl.BlockSpec(memory_space=pltpu.VMEM)
-    return pl.pallas_call(
+    scratch = [
+        pltpu.VMEM(queries.shape, BF16),
+        pltpu.VMEM(queries.shape, BF16),
+        pltpu.SemaphoreType.DMA((4,)),
+        pltpu.VMEM((shards,) + block, BF16),
+        pltpu.VMEM((nk * ny,) + block, BF16),
+        pltpu.VMEM((max(y_sends, 1),) + block, BF16),
+        pltpu.VMEM((max(nk - 1, 1),) + block, BF16),
+        pltpu.VMEM((2, qb * nnz + 1, BLK, HD), F32),
+        pltpu.VMEM((qb, nnz * BLK, H * BLK), F32),
+        pltpu.VMEM((qb, H * BLK, HD), BF16),
+        pltpu.VMEM((qb, H * BLK, HD), BF16),
+        pltpu.VMEM((qb, HD, H * BLK), BF16),
+        pltpu.VMEM((qb, HD, H * BLK), BF16),
+        pltpu.VMEM((qb, nnz * BLK, HD), BF16),
+        pltpu.VMEM((qb, nnz * BLK, HD), BF16),
+        pltpu.SMEM((qb, shards * kb), jnp.int32),
+        dma((nk - 1 + y_sends + nk * ny,)),
+        dma((shards,)),
+        dma((nk * ny,)),
+        dma((nk * ny,)),
+        dma((max(y_sends, 1),)),
+        dma((max(y_sends, 1),)),
+        dma((max(nk - 1, 1),)),
+        dma((max(nk - 1, 1),)),
+    ]
+    attended, grad_q, grad_k, grad_v = pl.pallas_call(
         functools.partial(kernel, nq, nk, nnz),
         out_shape=(
             jax.ShapeDtypeStruct(queries.shape, BF16),
             jax.ShapeDtypeStruct(queries.shape, BF16),
-            jax.ShapeDtypeStruct(keys.shape, BF16),
-            jax.ShapeDtypeStruct(keys.shape, BF16),
+            jax.ShapeDtypeStruct(tiles, BF16),
+            jax.ShapeDtypeStruct(tiles, BF16),
         ),
-        in_specs=[vmem] * 4 + [pl.BlockSpec(memory_space=pltpu.SMEM)],
+        in_specs=[pl.BlockSpec(memory_space=pltpu.HBM)] * 4 + [pl.BlockSpec(memory_space=pltpu.SMEM)],
         out_specs=(vmem,) * 4,
-        scratch_shapes=[
-            pltpu.VMEM((shards,) + block, BF16),
-            pltpu.VMEM((nk * ny,) + block, BF16),
-            pltpu.VMEM((max(y_sends, 1),) + block, BF16),
-            pltpu.VMEM((max(nk - 1, 1),) + block, BF16),
-            pltpu.VMEM((2, qb * nnz + 1, BLK, HD), F32),
-            pltpu.VMEM((qb, nnz * BLK, H * BLK), F32),
-            pltpu.VMEM((qb, H * BLK, HD), BF16),
-            pltpu.VMEM((qb, H * BLK, HD), BF16),
-            pltpu.VMEM((qb, HD, H * BLK), BF16),
-            pltpu.VMEM((qb, HD, H * BLK), BF16),
-            pltpu.VMEM((qb, nnz * BLK, HD), BF16),
-            pltpu.VMEM((qb, nnz * BLK, HD), BF16),
-            pltpu.SMEM((qb, shards * kb), jnp.int32),
-            dma((nk - 1 + y_sends + nk * ny,)),
-            dma((shards,)),
-            dma((nk * ny,)),
-            dma((nk * ny,)),
-            dma((max(y_sends, 1),)),
-            dma((max(y_sends, 1),)),
-            dma((max(nk - 1, 1),)),
-            dma((max(nk - 1, 1),)),
-        ],
+        scratch_shapes=scratch,
         compiler_params=pltpu.CompilerParams(
-            collective_id=0, has_side_effects=True, vmem_limit_bytes=58 * 1024 * 1024
+            collective_id=0, has_side_effects=True, vmem_limit_bytes=vmem_bytes(scratch, 4 * (queries.size + keys.size))
         ),
-    )(queries, out_grad, keys, values, pattern)
+    )(queries, out_grad, keys.reshape(tiles), values.reshape(tiles), pattern.T)
+    return attended, grad_q, grad_k.reshape(keys.shape), grad_v.reshape(keys.shape)
 
 
 def solution(mesh):

time: 56 us -> 56.5 us (level)
  local copies, waits for them, and re-layouts: 5.45 us -> 6.93 us
  Pallas kernels: 49.6 us -> 48.6 us
    unnamed x11 -> x14, local copies, waits for them, and re-layouts: 5.45 us -> 6.93 us
    pallas_call x1, Pallas kernels: 49.6 us -> 48.6 us  [body(): pl.pallas_call(functools.partial(kernel, nq, nk, nnz), out_shape=(jax.Sha...]
where the time goes in v3:
time: 56.5 us; the launch traced here: 56.2 us
  Pallas kernels  48.6 us (86%)
  local copies, waits for them, and re-layouts  6.93 us (12%)
  between operations  0.65 us (1%)
    pallas_call x1, Pallas kernels, body(): pl.pallas_call(functools.partial(kernel, nq, nk, nnz), out_shape=(jax.Sha...  48.6 us
    unnamed x14, local copies, waits for them, and re-layouts  6.93 us

profile of v3, /device:TPU:0, one launch (start us, length us, event | category | flops | bytes accessed | tf_op | source)
XLA Modules:
  0.0 56.2 jit_solution(7166806539588077107)
XLA Ops:
  0.6 0.0 copy-start
  0.6 0.9 %copy-done = bf16[256,512]{1,0:T(8,128)(2,1)S(1)} copy-done((bf16[256,512]{1,0:T(8,128)(2,1)S(1)}, bf16[256,512]{1,0:T(8,128)(2,1)}, u32[]{:S(2)}) %copy-start) | copy-done | bytes 262168
  1.6 0.0 copy-start.1
  1.6 0.9 %copy-done.1 = bf16[256,512]{1,0:T(8,128)(2,1)S(1)} copy-done((bf16[256,512]{1,0:T(8,128)(2,1)S(1)}, bf16[256,512]{1,0:T(8,128)(2,1)}, u32[]{:S(2)}) %copy-start.1) | copy-done | bytes 262168
  2.5 0.0 copy-start.2
  2.5 0.8 %copy-done.2 = bf16[256,128]{1,0:T(8,128)(2,1)S(1)} copy-done((bf16[256,128]{1,0:T(8,128)(2,1)S(1)}, bf16[256,128]{1,0:T(8,128)(2,1)}, u32[]{:S(2)}) %copy-start.2) | copy-done | bytes 65560
  3.4 0.0 copy-start.3
  3.4 0.8 %copy-done.3 = bf16[256,128]{1,0:T(8,128)(2,1)S(1)} copy-done((bf16[256,128]{1,0:T(8,128)(2,1)S(1)}, bf16[256,128]{1,0:T(8,128)(2,1)}, u32[]{:S(2)}) %copy-start.3) | copy-done | bytes 65560
  4.2 0.0 copy-start.4
  4.2 0.7 %copy-done.4 = s32[32,10]{0,1:T(8,128)S(1)} copy-done((s32[32,10]{0,1:T(8,128)S(1)}, s32[32,10]{0,1:T(8,128)}, u32[]{:S(2)}) %copy-start.4) | copy-done | bytes 1304
  4.9 48.6 %shard_map.84 = (bf16[256,512]{1,0:T(8,128)(2,1)S(1)}, bf16[256,512]{1,0:T(8,128)(2,1)S(1)}, bf16[2,128,128]{2,1,0:T(8,128)(2,1)S(1)}, bf16[2,128,128]{2,1,0:T(8,128)(2,1)S(1)}) custom-call(bf16[256,512]{1,0:T(8,128)(2,1)S(1)} %copy-done, bf16[256,512]{1,0:T(8,128)(2,1)S(1)} %copy-done.1, bf16[2,128,128]{2,1,0:T(8,128)(2,1)S(1)} %bitcast.7, ...), custom_call_target="tpu_custom_call" | custom-call | tf_op jit(solution)/shard_map/pallas_call | solution.py:331
  53.5 0.7 %copy.13 = bf16[256,512]{1,0:T(8,128)(2,1)} copy(bf16[256,512]{1,0:T(8,128)(2,1)S(1)} %get-tuple-element.16) | data formatting | bytes 524288
  54.2 0.7 %copy.14 = bf16[256,512]{1,0:T(8,128)(2,1)} copy(bf16[256,512]{1,0:T(8,128)(2,1)S(1)} %get-tuple-element.17) | data formatting | bytes 524288
  54.9 0.6 %copy.15 = bf16[256,128]{1,0:T(8,128)(2,1)} copy(bf16[256,128]{1,0:T(8,128)(2,1)S(1)} %bitcast.6) | data formatting | bytes 131072
  55.6 0.6 %copy.16 = bf16[256,128]{1,0:T(8,128)(2,1)} copy(bf16[256,128]{1,0:T(8,128)(2,1)S(1)} %bitcast.5) | data formatting | bytes 131072
Async XLA Ops:
  0.6 1.0 %copy-start = (bf16[256,512]{1,0:T(8,128)(2,1)S(1)}, bf16[256,512]{1,0:T(8,128)(2,1)}, u32[]{:S(2)}) copy-start(bf16[256,512]{1,0:T(8,128)(2,1)} %q_hbm.1) | copy-start | bytes 786436
  1.6 0.9 %copy-start.1 = (bf16[256,512]{1,0:T(8,128)(2,1)S(1)}, bf16[256,512]{1,0:T(8,128)(2,1)}, u32[]{:S(2)}) copy-start(bf16[256,512]{1,0:T(8,128)(2,1)} %g_hbm.1) | copy-start | bytes 786436
  2.5 0.8 %copy-start.2 = (bf16[256,128]{1,0:T(8,128)(2,1)S(1)}, bf16[256,128]{1,0:T(8,128)(2,1)}, u32[]{:S(2)}) copy-start(bf16[256,128]{1,0:T(8,128)(2,1)} %param.6) | copy-start | bytes 196612
  3.4 0.8 %copy-start.3 = (bf16[256,128]{1,0:T(8,128)(2,1)S(1)}, bf16[256,128]{1,0:T(8,128)(2,1)}, u32[]{:S(2)}) copy-start(bf16[256,128]{1,0:T(8,128)(2,1)} %param.7) | copy-start | bytes 196612
  4.2 0.7 %copy-start.4 = (s32[32,10]{0,1:T(8,128)S(1)}, s32[32,10]{0,1:T(8,128)}, u32[]{:S(2)}) copy-start(s32[32,10]{0,1:T(8,128)} %param.9) | copy-start | bytes 3844
